TPU v7x, 32 devices: a whole 2x2x4 slice. The times are simulated.
32 devices in a mesh: grp: 2 (over y), sp: 4 (over z), sec: 2 (over x), mb: 2 (over core).
Axes of the slice: x: 2, y: 2, z: 4, core: 2. Of those that a mesh axis runs over, the one named last changes fastest.
Arguments:
- atmosphere: bfloat16 [8, 24, 32, 256], P(('grp', 'mb'), None, 'sp', 'sec'), parts along dimension 0, may hold values from -6 to 6
- ocean_state: bfloat16 [8, 8, 32, 128], P(('grp', 'mb'), None, 'sp'), parts along dimension 0, may hold values from -6 to 6
- fluxes: bfloat16 [8, 8, 32, 128], P(('grp', 'mb'), None, 'sp'), parts along dimension 0, may hold values from -6 to 6
- sea_mask: int32 [32, 128], P('sp'), may hold values 0 or 1
- air_entry: bfloat16 [3, 3, 32, 136], replicated, may hold values from -0.375 to 0.375
- air_middle: bfloat16 [3, 3, 136, 136], replicated, may hold values from -0.15625 to 0.15625
- air_exit: bfloat16 [3, 3, 136, 32], replicated, may hold values from -0.15625 to 0.15625
- sea_entry: bfloat16 [3, 3, 16, 136], replicated, may hold values from -0.5 to 0.5
- sea_exit: bfloat16 [3, 3, 136, 8], replicated, may hold values from -0.15625 to 0.15625
Outputs:
- air_final: bfloat16 [8, 24, 32, 256], P(('grp', 'mb'), None, 'sp', 'sec'), parts along dimension 0
- sea_final: bfloat16 [8, 8, 32, 128], P(('grp', 'mb'), None, 'sp'), parts along dimension 0
There are 2 independent parts, one for each index of `grp`. A program takes and returns all parts, laid end to end along the dimension named above; an argument that names none is the same for every part. Nothing has to cross between parts.
All inputs are finite; a program needn't handle non-finite values. No bound on the sum of `sea_mask` on one device may be relied on, other than what follows from the above.
Results may differ from a plain program's by a relative error of at most 0.0055.
Values may be sent and summed in bfloat16 or wider, within the bound.
No kernel may reach another device: no remote copies, remote signals or barrier semaphores. Data moves between devices by JAX's collectives and lax.ppermute only.
A program may use at most 64 MiB of HBM per device.

v0:
```python
import jax
import jax.numpy as jnp
from jax import lax
from jax.sharding import PartitionSpec as P

STEPS = 2
dilations = (1, 2, 4)


def with_halo(block, sides, width):
    for axis, dim in sides:
        count = lax.axis_size(axis)
        forward = [(i, i + 1) for i in range(count - 1)]
        forward.append((count - 1, 0))
        backward = [(target, source) for source, target in forward]
        low = lax.ppermute(
            lax.slice_in_dim(block, block.shape[dim] - width, None, axis=dim), axis, forward
        )
        high = lax.ppermute(lax.slice_in_dim(block, 0, width, axis=dim), axis, backward)
        block = jnp.concatenate([low, block, high], axis=dim)
    return block


def spread_2(value, axis, source):
    kept = jnp.where(lax.axis_index(axis) == source, value, 0).astype(value.dtype)
    return lax.psum(kept, axis)


def tap_sum(source, weight, dilation):
    out_rows = source.shape[2] - 2 * dilation
    out_cols = source.shape[3] - 2 * dilation
    pieces = []
    for tap_row in range(3):
        for tap_col in range(3):
            sliced = lax.slice_in_dim(
                source, tap_row * dilation, tap_row * dilation + out_rows, axis=2
            )
            sliced = lax.slice_in_dim(
                sliced, tap_col * dilation, tap_col * dilation + out_cols, axis=3
            )
            pieces.append(sliced)
    stacked = jnp.concatenate(pieces, axis=1)
    flat_weight = weight.reshape(-1, weight.shape[3])
    return jnp.einsum("mkrc,ko->morc", stacked, flat_weight, preferred_element_type=jnp.float32)


def gelu_round(values):
    return jax.nn.gelu(values, approximate=True).astype(jnp.bfloat16)


def keep_columns(block, first_column, limit):
    columns = lax.iota(jnp.int32, block.shape[3]) + first_column
    inside = (columns >= 0) & (columns < limit)
    return jnp.where(inside[None, None, None, :], block, jnp.zeros_like(block))


def shards(
    atmosphere, ocean_state, fluxes, sea_mask, air_entry, air_middle, air_exit, sea_entry, sea_exit
):
    sections = lax.axis_size("sec")
    position = lax.axis_index("sec")
    is_ocean = position == sections - 1
    band_cols = atmosphere.shape[3]
    ocean_cols = ocean_state.shape[3]
    field_count = atmosphere.shape[1]
    sea_weight = sea_mask.astype(jnp.float32)
    air_weights = (air_entry, air_middle, air_exit)
    sea_weights = (sea_entry, sea_exit)

    def air_layer(extended, layer_index):
        produced = tap_sum(extended, air_weights[layer_index], dilations[layer_index])
        if layer_index < 2:
            return gelu_round(produced)
        return produced

    def air_blank(extended, layer_index):
        spread = dilations[layer_index]
        out_shape = (
            extended.shape[0],
            air_weights[layer_index].shape[3],
            extended.shape[2] - 2 * spread,
            extended.shape[3] - 2 * spread,
        )
        return jnp.zeros(out_shape, jnp.bfloat16 if layer_index < 2 else jnp.float32)

    def sea_layer(extended, layer_index):
        padded = jnp.pad(extended, ((0, 0), (0, 0), (0, 0), (1, 1)))
        produced = tap_sum(padded, sea_weights[layer_index], 1)
        if layer_index < 1:
            return gelu_round(produced)
        return produced

    def sea_blank(extended, layer_index):
        out_shape = (
            extended.shape[0],
            sea_weights[layer_index].shape[3],
            extended.shape[2] - 2,
            ocean_cols,
        )
        return jnp.zeros(out_shape, jnp.bfloat16 if layer_index < 1 else jnp.float32)

    def air_extend(current, layer_index, margin):
        extended = with_halo(current, (("sp", 2), ("sec", 3)), dilations[layer_index])
        margin = dilations[layer_index]
        limit = band_cols * sections if layer_index == 0 else ocean_cols
        extended = keep_columns(extended, position * band_cols - margin, limit)
        return (extended, margin - dilations[layer_index])

    def sea_extend(current):
        return with_halo(current, (("sp", 2),), 1)

    def run_segment(air_job, sea_job):
        air_current = None
        sea_current = None
        margin = 0
        if air_job is not None:
            air_current = jnp.concatenate(air_job, axis=1)
        if sea_job is not None:
            sea_current = jnp.concatenate(sea_job, axis=1)
        for layer_index in range(3):
            air_ready = None
            sea_ready = None
            if air_current is not None:
                air_ready, margin = air_extend(air_current, layer_index, margin)
            if sea_current is not None and layer_index < 2:
                sea_ready = sea_extend(sea_current)
            if air_ready is None and sea_ready is None:
                continue

            def on_sea(ready):
                air_given, sea_given = ready
                air_made = None if air_given is None else air_blank(air_given, layer_index)
                sea_made = None if sea_given is None else sea_layer(sea_given, layer_index)
                return (air_made, sea_made)

            def on_air(ready):
                air_given, sea_given = ready
                air_made = None if air_given is None else air_layer(air_given, layer_index)
                sea_made = None if sea_given is None else sea_blank(sea_given, layer_index)
                return (air_made, sea_made)

            air_next, sea_next = lax.cond(is_ocean, on_sea, on_air, (air_ready, sea_ready))
            if air_ready is not None:
                air_current = air_next
            if sea_ready is not None:
                sea_current = sea_next
        air_result = None
        sea_result = None
        if air_job is not None:
            previous = air_job[0]
            renewed = (previous.astype(jnp.float32) + air_current[:, :field_count]).astype(
                jnp.bfloat16
            )
            air_result = (renewed, air_current[:, field_count:].astype(jnp.bfloat16))
        if sea_job is not None:
            previous = sea_job[0]
            sea_result = (
                previous.astype(jnp.float32) + sea_weight[None, None] * sea_current
            ).astype(jnp.bfloat16)
        return (air_result, sea_result)

    air_now, sea_now, flux_now = (atmosphere, ocean_state, fluxes)
    for step_index in range(STEPS):
        sea_now = run_segment(None, (sea_now, flux_now))[1]
        shared = spread_2(sea_now, "sec", sections - 1)
        start_col = jnp.minimum(position, sections - 2) * band_cols
        own_band = lax.dynamic_slice_in_dim(shared, start_col, band_cols, 3)
        own_band = jnp.where(is_ocean, jnp.zeros_like(own_band), own_band)
        sea_now = shared
        air_now, flux_band = run_segment((air_now, own_band), None)[0]
        if step_index + 1 < STEPS:
            collected = lax.all_gather(flux_band, "sec", axis=3, tiled=True)
            flux_now = collected[:, :, :, :ocean_cols]
    return (air_now, sea_now)


def solution(mesh):
    placed = (
        P(("grp", "mb"), None, "sp", "sec"),
        P(("grp", "mb"), None, "sp", None),
        P(("grp", "mb"), None, "sp", None),
        P("sp", None),
        P(),
        P(),
        P(),
        P(),
        P(),
    )
    return jax.shard_map(
        shards,
        mesh=mesh,
        in_specs=placed,
        out_specs=(P(("grp", "mb"), None, "sp", "sec"), P(("grp", "mb"), None, "sp", None)),
        check_vma=False,
    )
```

profile of v0, /device:TPU:0, one launch (start us, length us, event | category | flops | bytes accessed | tf_op | source)
XLA Modules:
  0.0 245.5 jit_solution(14746877766434007346)
XLA Ops:
  2.2 3.1 %collective-permute-start = (bf16[2,16,1,128]{3,1,2,0:T(8,128)(2,1)S(1)}, bf16[2,16,1,128]{3,1,2,0:T(8,128)(2,1)S(1)}, u32[]{:S(2)}, u32[]{:S(2)}) collective-permute-start(bf16[2,16,1,128]{3,1,2,0:T(8,128)(2,1)S(1)} %get-tuple-element.252), channel_id=1, source_target_pairs={{0,4},{4,8},{8,12},{12,0},{1,5},{5,9},{9,13},{13,1},{2,6},{6,10},{... | collective-permute-start | bytes 24584 | tf_op jit(solution)/shard_map/ppermute | solution.py:16
  16.7 17.5 %psum.14 = bf16[2,8,8,128]{3,2,1,0:T(8,128)(2,1)S(1)} all-reduce(bf16[2,8,8,128]{3,2,1,0:T(8,128)(2,1)S(1)} %fusion.76), channel_id=1, replica_groups=mesh['grp'=2,'sp'=4,'sec'=2,'mb'=2] {'sec'}, use_global_device_ids=true, to_apply=%region_4.5 | all-reduce | flops 16384 | bytes 65536 | tf_op jit(solution)/shard_map/psum | solution.py:26
  35.3 2.8 %collective-permute-start.5 = (bf16[2,32,1,128]{3,1,2,0:T(8,128)(2,1)S(1)}, bf16[2,32,1,128]{3,1,2,0:T(8,128)(2,1)S(1)}, u32[]{:S(2)}, u32[]{:S(2)}) collective-permute-start(bf16[2,32,1,128]{3,1,2,0:T(8,128)(2,1)S(1)} %get-tuple-element.249), channel_id=1, source_target_pairs={{4,0},{8,4},{12,8},{0,12},{5,1},{9,5},{13,9},{1,13},{6,2},{10,6},{... | collective-permute-start | bytes 49160 | tf_op jit(solution)/shard_map/ppermute | solution.py:19
  42.6 2.8 %collective-permute-done.6 = bf16[2,32,10,1]{3,1,2,0:T(8,128)(2,1)S(1)} collective-permute-done((bf16[2,32,10,1]{3,1,2,0:T(8,128)(2,1)S(1)}, bf16[2,32,10,1]{3,1,2,0:T(8,128)(2,1)S(1)}, u32[]{:S(2)}, u32[]{:S(2)}) %collective-permute-start.6) | collective-permute-done | bytes 1312 | tf_op jit(solution)/shard_map/ppermute | solution.py:16
  51.4 2.8 %collective-permute-start.9 = (bf16[2,136,2,128]{1,3,2,0:T(8,128)(2,1)S(1)}, bf16[2,136,2,128]{1,3,2,0:T(8,128)(2,1)S(1)}, u32[]{:S(2)}, u32[]{:S(2)}) collective-permute-start(bf16[2,136,2,128]{1,3,2,0:T(8,128)(2,1)S(1)} %get-tuple-element.237), channel_id=1, source_target_pairs={{4,0},{8,4},{12,8},{0,12},{5,1},{9,5},{13,9},{1,13},{6,2},{10,6},{... | collective-permute-start | bytes 417800 | tf_op jit(solution)/shard_map/ppermute | solution.py:19
  54.2 4.4 %collective-permute-done.8 = bf16[2,136,2,128]{1,3,2,0:T(8,128)(2,1)S(1)} collective-permute-done((bf16[2,136,2,128]{1,3,2,0:T(8,128)(2,1)S(1)}, bf16[2,136,2,128]{1,3,2,0:T(8,128)(2,1)S(1)}, u32[]{:S(2)}, u32[]{:S(2)}) %collective-permute-start.8) | collective-permute-done | bytes 139296 | tf_op jit(solution)/shard_map/ppermute | solution.py:16
  67.8 8.1 %conditional.13 = (bf16[2,136,8,128]{3,1,2,0:T(8,128)(2,1)S(1)}) conditional(s32[]{:T(128)} %convert_element_type.68, (pred[132]{0:T(512)(128)(4,1)S(1)}, bf16[2,136,12,132]{1,3,2,0:T(8,128)(2,1)S(1)}, bf16[2,136,12,132]{3,1,2,0:T(8,128)(2,1)}, bf16[3,3,136,136]{3,2,1,0:T(8,128)(2,1)}) %tuple.76, () %tuple.77), branch_computations={%region_7.8_spmd, %region_8.9_spmd} | conditional | flops 684774144 | bytes 21570856 | solution.py:142
  81.8 9.6 %collective-permute-done.12 = bf16[2,136,4,128]{1,2,3,0:T(4,128)(2,1)S(1)} collective-permute-done((bf16[2,136,4,128]{1,2,3,0:T(4,128)(2,1)}, bf16[2,136,4,128]{1,2,3,0:T(4,128)(2,1)S(1)}, u32[]{:S(2)}, u32[]{:S(2)}) %collective-permute-start.12) | collective-permute-done | bytes 278560 | tf_op jit(solution)/shard_map/ppermute | solution.py:16
  91.3 5.3 %collective-permute-done.13 = bf16[2,136,4,128]{1,2,3,0:T(4,128)(2,1)S(1)} collective-permute-done((bf16[2,136,4,128]{1,2,3,0:T(4,128)(2,1)S(1)}, bf16[2,136,4,128]{1,2,3,0:T(4,128)(2,1)S(1)}, u32[]{:S(2)}, u32[]{:S(2)}) %collective-permute-start.13) | collective-permute-done | bytes 278560 | tf_op jit(solution)/shard_map/ppermute | solution.py:19
  101.8 2.6 %pad_maximum_fusion = bf16[2,136,16,136]{1,2,3,0:T(8,128)(2,1)} fusion(bf16[2,136,16,4]{1,2,3,0:T(8,128)(2,1)S(1)} %collective-permute-done.15, bf16[2,136,4,128]{1,2,3,0:T(4,128)(2,1)S(1)} %collective-permute-done.13, bf16[2,136,8,128]{1,2,3,0:T(8,128)(2,1)S(1)} %copy.69, bf16[2,136,4,128]{1,2,3,0:T(4,128)(2,1)S(1)} %collective-permute-done.12, ...), kind=kLoop, calls=%fused_computation.188 | loop fusion | flops 5918720 | bytes 2367488 | tf_op jit(solution)/shard_map/concatenate | solution.py:20
  105.3 14.8 %conditional.14 = (f32[2,32,8,128]{3,2,1,0:T(8,128)S(1)}, f32[2,24,8,128]{3,2,1,0:T(8,128)S(1)}) conditional(s32[]{:T(128)} %convert_element_type.68, (pred[136]{0:T(512)(128)(4,1)S(1)}, bf16[2,136,16,136]{1,2,3,0:T(8,128)(2,1)}, bf16[2,136,16,136]{3,1,2,0:T(8,128)(2,1)S(1)}, bf16[3,3,136,32]{2,3,1,0:T(8,128)(2,1)S(1)}) %tuple.159, () %tuple.79), branch_computations={%region_9.10_spmd, %region_10.11_spmd} | conditional | flops 161024000 | bytes 42584756 | solution.py:142
  105.3 4.6 %copy.72 = bf16[2,136,16,136]{3,1,2,0:T(8,128)(2,1)} copy(bf16[2,136,16,136]{1,2,3,0:T(8,128)(2,1)} %get-tuple-element.198) | data formatting | bytes 2367488 | tf_op jit(solution)/shard_map
  116.6 3.4 %convolution_bitcast_fusion.4 = f32[2,32,8,128]{3,1,2,0:T(8,128)S(1)} fusion(bf16[2,1224,8,128]{3,1,2,0:T(8,128)(2,1)} %copy-done.2, bf16[1224,32,1,1]{0,1,2,3:T(8,128)(2,1)S(1)} %reshape.60), kind=kOutput, calls=%fused_computation.83 | convolution fusion | flops 160432128 | bytes 5353984 | tf_op jit(solution)/shard_map/cond/branch_0_fun/mkrc,ko->morc/dot_general | solution.py:44
  120.1 4.6 %all_gather.3 = bf16[2,8,8,256]{3,2,1,0:T(8,128)(2,1)S(1)} all-gather(bf16[2,8,8,128]{3,2,1,0:T(8,128)(2,1)S(1)} %slice.832), channel_id=1, replica_groups=mesh['grp'=2,'sp'=4,'sec'=2,'mb'=2] {'sec'}, dimensions={3}, use_global_device_ids=true | all-gather | bytes 98304 | tf_op jit(solution)/shard_map/all_gather | solution.py:172
  125.1 3.5 %collective-permute-start.17 = (bf16[2,16,1,128]{3,2,1,0:T(2,128)(2,1)S(1)}, bf16[2,16,1,128]{3,2,1,0:T(2,128)(2,1)S(1)}, u32[]{:S(2)}, u32[]{:S(2)}) collective-permute-start(bf16[2,16,1,128]{3,2,1,0:T(2,128)(2,1)S(1)} %get-tuple-element.251), channel_id=1, source_target_pairs={{4,0},{8,4},{12,8},{0,12},{5,1},{9,5},{13,9},{1,13},{6,2},{10,6},{... | collective-permute-start | bytes 24584 | tf_op jit(solution)/shard_map/ppermute | solution.py:19
  132.4 4.0 %collective-permute-start.19 = (bf16[2,136,1,128]{3,1,2,0:T(8,128)(2,1)S(1)}, bf16[2,136,1,128]{3,1,2,0:T(8,128)(2,1)S(1)}, u32[]{:S(2)}, u32[]{:S(2)}) collective-permute-start(bf16[2,136,1,128]{3,1,2,0:T(8,128)(2,1)S(1)} %get-tuple-element.239), channel_id=1, source_target_pairs={{4,0},{8,4},{12,8},{0,12},{5,1},{9,5},{13,9},{1,13},{6,2},{10,6},{... | collective-permute-start | bytes 208904 | tf_op jit(solution)/shard_map/ppermute | solution.py:19
  140.5 15.9 %psum.15 = bf16[2,8,8,128]{3,2,1,0:T(8,128)(2,1)S(1)} all-reduce(bf16[2,8,8,128]{3,2,1,0:T(8,128)(2,1)S(1)} %fusion.77), channel_id=1, replica_groups=mesh['grp'=2,'sp'=4,'sec'=2,'mb'=2] {'sec'}, use_global_device_ids=true, to_apply=%region_15.16 | all-reduce | flops 16384 | bytes 65536 | tf_op jit(solution)/shard_map/psum | solution.py:26
  157.9 2.6 %collective-permute-start.21 = (bf16[2,32,1,128]{3,2,1,0:T(2,128)(2,1)S(1)}, bf16[2,32,1,128]{3,2,1,0:T(2,128)(2,1)S(1)}, u32[]{:S(2)}, u32[]{:S(2)}) collective-permute-start(bf16[2,32,1,128]{3,2,1,0:T(2,128)(2,1)S(1)} %get-tuple-element.247), channel_id=1, source_target_pairs={{4,0},{8,4},{12,8},{0,12},{5,1},{9,5},{13,9},{1,13},{6,2},{10,6},{... | collective-permute-start | bytes 49160 | tf_op jit(solution)/shard_map/ppermute | solution.py:19
  164.8 4.3 %collective-permute-done.22 = bf16[2,32,10,1]{3,2,1,0:T(8,128)(2,1)S(1)} collective-permute-done((bf16[2,32,10,1]{3,2,1,0:T(8,128)(2,1)S(1)}, bf16[2,32,10,1]{3,2,1,0:T(8,128)(2,1)S(1)}, u32[]{:S(2)}, u32[]{:S(2)}) %collective-permute-start.22) | collective-permute-done | bytes 1312 | tf_op jit(solution)/shard_map/ppermute | solution.py:16
  169.1 2.8 %collective-permute-done.23 = bf16[2,32,10,1]{3,2,1,0:T(8,128)(2,1)S(1)} collective-permute-done((bf16[2,32,10,1]{3,2,1,0:T(8,128)(2,1)S(1)}, bf16[2,32,10,1]{3,2,1,0:T(8,128)(2,1)S(1)}, u32[]{:S(2)}, u32[]{:S(2)}) %collective-permute-start.23) | collective-permute-done | bytes 1312 | tf_op jit(solution)/shard_map/ppermute | solution.py:19
  172.5 2.7 %conditional.17 = (bf16[2,136,8,128]{3,1,2,0:T(8,128)(2,1)S(1)}) conditional(s32[]{:T(128)} %convert_element_type.68, (pred[130]{0:T(512)(128)(4,1)}, bf16[2,32,10,130]{3,2,1,0:T(8,128)(2,1)S(1)}, bf16[2,32,10,130]{3,1,2,0:T(8,128)(2,1)S(1)}, bf16[3,3,32,136]{3,2,1,0:T(8,128)(2,1)}) %tuple.84, () %tuple.85), branch_computations={%region_16.17_spmd, %region_17.18_spmd} | conditional | flops 163022080 | bytes 4987046 | solution.py:142
  178.8 2.7 %collective-permute-start.25 = (bf16[2,136,2,128]{1,3,2,0:T(8,128)(2,1)S(1)}, bf16[2,136,2,128]{1,3,2,0:T(8,128)(2,1)S(1)}, u32[]{:S(2)}, u32[]{:S(2)}) collective-permute-start(bf16[2,136,2,128]{1,3,2,0:T(8,128)(2,1)S(1)} %get-tuple-element.233), channel_id=1, source_target_pairs={{4,0},{8,4},{12,8},{0,12},{5,1},{9,5},{13,9},{1,13},{6,2},{10,6},{... | collective-permute-start | bytes 417800 | tf_op jit(solution)/shard_map/ppermute | solution.py:19
  181.5 4.4 %collective-permute-done.24 = bf16[2,136,2,128]{1,3,2,0:T(8,128)(2,1)S(1)} collective-permute-done((bf16[2,136,2,128]{1,3,2,0:T(8,128)(2,1)S(1)}, bf16[2,136,2,128]{1,3,2,0:T(8,128)(2,1)S(1)}, u32[]{:S(2)}, u32[]{:S(2)}) %collective-permute-start.24) | collective-permute-done | bytes 139296 | tf_op jit(solution)/shard_map/ppermute | solution.py:16
  194.1 9.4 %conditional.18 = (bf16[2,136,8,128]{3,1,2,0:T(8,128)(2,1)S(1)}) conditional(s32[]{:T(128)} %convert_element_type.68, (pred[132]{0:T(512)(128)(4,1)S(1)}, bf16[2,136,12,132]{1,3,2,0:T(8,128)(2,1)}, bf16[2,136,12,132]{3,1,2,0:T(8,128)(2,1)}, bf16[3,3,136,136]{3,2,1,0:T(8,128)(2,1)}) %tuple.164, () %tuple.87), branch_computations={%region_18.19_spmd, %region_19.20_spmd} | conditional | flops 684774144 | bytes 21570856 | solution.py:142
  194.1 3.8 %copy.83 = bf16[2,136,12,132]{3,1,2,0:T(8,128)(2,1)} copy(bf16[2,136,12,132]{1,3,2,0:T(8,128)(2,1)} %get-tuple-element.210) | data formatting | bytes 1723392 | tf_op jit(solution)/shard_map
  207.7 2.7 %collective-permute-start.29 = (bf16[2,136,4,128]{1,2,3,0:T(4,128)(2,1)S(1)}, bf16[2,136,4,128]{1,2,3,0:T(4,128)(2,1)S(1)}, u32[]{:S(2)}, u32[]{:S(2)}) collective-permute-start(bf16[2,136,4,128]{1,2,3,0:T(4,128)(2,1)S(1)} %get-tuple-element.231), channel_id=1, source_target_pairs={{4,0},{8,4},{12,8},{0,12},{5,1},{9,5},{13,9},{1,13},{6,2},{10,6},{... | collective-permute-start | bytes 835592 | tf_op jit(solution)/shard_map/ppermute | solution.py:19
  210.3 7.3 %collective-permute-done.28 = bf16[2,136,4,128]{1,2,3,0:T(4,128)(2,1)S(1)} collective-permute-done((bf16[2,136,4,128]{1,2,3,0:T(4,128)(2,1)S(1)}, bf16[2,136,4,128]{1,2,3,0:T(4,128)(2,1)S(1)}, u32[]{:S(2)}, u32[]{:S(2)}) %collective-permute-start.28) | collective-permute-done | bytes 278560 | tf_op jit(solution)/shard_map/ppermute | solution.py:16
  217.6 4.9 %collective-permute-done.29 = bf16[2,136,4,128]{1,2,3,0:T(4,128)(2,1)S(1)} collective-permute-done((bf16[2,136,4,128]{1,2,3,0:T(4,128)(2,1)S(1)}, bf16[2,136,4,128]{1,2,3,0:T(4,128)(2,1)S(1)}, u32[]{:S(2)}, u32[]{:S(2)}) %collective-permute-start.29) | collective-permute-done | bytes 278560 | tf_op jit(solution)/shard_map/ppermute | solution.py:19
  227.6 2.6 %pad_maximum_fusion.1 = bf16[2,136,16,136]{1,2,3,0:T(8,128)(2,1)} fusion(bf16[2,136,16,4]{1,2,3,0:T(8,128)(2,1)S(1)} %collective-permute-done.31, bf16[2,136,4,128]{1,2,3,0:T(4,128)(2,1)S(1)} %collective-permute-done.29, bf16[2,136,8,128]{1,2,3,0:T(8,128)(2,1)S(1)} %copy.84, bf16[2,136,4,128]{1,2,3,0:T(4,128)(2,1)S(1)} %collective-permute-done.28, ...), kind=kLoop, calls=%fused_computation.189 | loop fusion | flops 5918720 | bytes 2367488 | tf_op jit(solution)/shard_map/concatenate | solution.py:20
  230.2 14.7 %conditional.19 = (f32[2,24,8,128]{3,2,1,0:T(8,128)S(1)}) conditional(s32[]{:T(128)} %convert_element_type.68, (pred[136]{0:T(512)(128)(4,1)S(1)}, bf16[2,136,16,136]{1,2,3,0:T(8,128)(2,1)}, bf16[2,136,16,136]{3,1,2,0:T(8,128)(2,1)S(1)}, bf16[3,3,136,32]{2,3,1,0:T(8,128)(2,1)S(1)}) %tuple.163, () %tuple.89), branch_computations={%region_20.21_spmd, %region_21.22_spmd} | conditional | flops 161024000 | bytes 42453676 | solution.py:142
  230.2 4.6 %copy.87 = bf16[2,136,16,136]{3,1,2,0:T(8,128)(2,1)} copy(bf16[2,136,16,136]{1,2,3,0:T(8,128)(2,1)} %get-tuple-element.214) | data formatting | bytes 2367488 | tf_op jit(solution)/shard_map
  241.4 3.4 %convolution_bitcast_fusion.9 = f32[2,32,8,128]{3,1,2,0:T(8,128)S(1)} fusion(bf16[2,1224,8,128]{3,1,2,0:T(8,128)(2,1)} %copy-done.3, bf16[1224,32,1,1]{0,1,2,3:T(8,128)(2,1)S(1)} %reshape.65), kind=kOutput, calls=%fused_computation.177 | convolution fusion | flops 160432128 | bytes 5353984 | tf_op jit(solution)/shard_map/cond/branch_0_fun/mkrc,ko->morc/dot_general | solution.py:44
  (224 shorter events, 113.8 us)
Async XLA Ops:
  2.2 6.8 %collective-permute-start = (bf16[2,16,1,128]{3,1,2,0:T(8,128)(2,1)S(1)}, bf16[2,16,1,128]{3,1,2,0:T(8,128)(2,1)S(1)}, u32[]{:S(2)}, u32[]{:S(2)}) collective-permute-start(bf16[2,16,1,128]{3,1,2,0:T(8,128)(2,1)S(1)} %get-tuple-element.252), channel_id=1, source_target_pairs={{0,4},{4,8},{8,12},{12,0},{1,5},{5,9},{9,13},{13,1},{2,6},{6,10},{... | collective-permute-start | bytes 24584 | tf_op jit(solution)/shard_map/ppermute | solution.py:16
  5.3 3.7 %collective-permute-start.1 = (bf16[2,16,1,128]{3,1,2,0:T(8,128)(2,1)S(1)}, bf16[2,16,1,128]{3,1,2,0:T(8,128)(2,1)S(1)}, u32[]{:S(2)}, u32[]{:S(2)}) collective-permute-start(bf16[2,16,1,128]{3,1,2,0:T(8,128)(2,1)S(1)} %get-tuple-element.253), channel_id=1, source_target_pairs={{4,0},{8,4},{12,8},{0,12},{5,1},{9,5},{13,9},{1,13},{6,2},{10,6},{... | collective-permute-start | bytes 24584 | tf_op jit(solution)/shard_map/ppermute | solution.py:19
  9.2 6.4 %collective-permute-start.2 = (bf16[2,136,1,128]{3,1,2,0:T(8,128)(2,1)S(1)}, bf16[2,136,1,128]{3,1,2,0:T(8,128)(2,1)S(1)}, u32[]{:S(2)}, u32[]{:S(2)}) collective-permute-start(bf16[2,136,1,128]{3,1,2,0:T(8,128)(2,1)S(1)} %get-tuple-element.240), channel_id=1, source_target_pairs={{0,4},{4,8},{8,12},{12,0},{1,5},{5,9},{9,13},{13,1},{2,6},{6,10},{... | collective-permute-start | bytes 208904 | tf_op jit(solution)/shard_map/ppermute | solution.py:16
  10.7 5.1 %collective-permute-start.3 = (bf16[2,136,1,128]{3,1,2,0:T(8,128)(2,1)S(1)}, bf16[2,136,1,128]{3,1,2,0:T(8,128)(2,1)S(1)}, u32[]{:S(2)}, u32[]{:S(2)}) collective-permute-start(bf16[2,136,1,128]{3,1,2,0:T(8,128)(2,1)S(1)} %get-tuple-element.241), channel_id=1, source_target_pairs={{4,0},{8,4},{12,8},{0,12},{5,1},{9,5},{13,9},{1,13},{6,2},{10,6},{... | collective-permute-start | bytes 208904 | tf_op jit(solution)/shard_map/ppermute | solution.py:19
  34.2 5.6 %collective-permute-start.4 = (bf16[2,32,1,128]{3,1,2,0:T(8,128)(2,1)S(1)}, bf16[2,32,1,128]{3,1,2,0:T(8,128)(2,1)S(1)}, u32[]{:S(2)}, u32[]{:S(2)}) collective-permute-start(bf16[2,32,1,128]{3,1,2,0:T(8,128)(2,1)S(1)} %get-tuple-element.248), channel_id=1, source_target_pairs={{0,4},{4,8},{8,12},{12,0},{1,5},{5,9},{9,13},{13,1},{2,6},{6,10},{... | collective-permute-start | bytes 49160 | tf_op jit(solution)/shard_map/ppermute | solution.py:16
  35.3 4.5 %collective-permute-start.5 = (bf16[2,32,1,128]{3,1,2,0:T(8,128)(2,1)S(1)}, bf16[2,32,1,128]{3,1,2,0:T(8,128)(2,1)S(1)}, u32[]{:S(2)}, u32[]{:S(2)}) collective-permute-start(bf16[2,32,1,128]{3,1,2,0:T(8,128)(2,1)S(1)} %get-tuple-element.249), channel_id=1, source_target_pairs={{4,0},{8,4},{12,8},{0,12},{5,1},{9,5},{13,9},{1,13},{6,2},{10,6},{... | collective-permute-start | bytes 49160 | tf_op jit(solution)/shard_map/ppermute | solution.py:19
  40.0 5.4 %collective-permute-start.6 = (bf16[2,32,10,1]{3,1,2,0:T(8,128)(2,1)S(1)}, bf16[2,32,10,1]{3,1,2,0:T(8,128)(2,1)S(1)}, u32[]{:S(2)}, u32[]{:S(2)}) collective-permute-start(bf16[2,32,10,1]{3,1,2,0:T(8,128)(2,1)S(1)} %get-tuple-element.244), channel_id=1, source_target_pairs={{0,2},{2,0},{1,3},{3,1},{4,6},{6,4},{5,7},{7,5},{8,10},{10,8},{9,1... | collective-permute-start | bytes 3848 | tf_op jit(solution)/shard_map/ppermute | solution.py:16
  40.1 7.0 %collective-permute-start.7 = (bf16[2,32,10,1]{3,1,2,0:T(8,128)(2,1)S(1)}, bf16[2,32,10,1]{3,1,2,0:T(8,128)(2,1)S(1)}, u32[]{:S(2)}, u32[]{:S(2)}) collective-permute-start(bf16[2,32,10,1]{3,1,2,0:T(8,128)(2,1)S(1)} %get-tuple-element.245), channel_id=1, source_target_pairs={{2,0},{0,2},{3,1},{1,3},{6,4},{4,6},{7,5},{5,7},{10,8},{8,10},{11,... | collective-permute-start | bytes 3848 | tf_op jit(solution)/shard_map/ppermute | solution.py:19
  50.2 8.3 %collective-permute-start.8 = (bf16[2,136,2,128]{1,3,2,0:T(8,128)(2,1)S(1)}, bf16[2,136,2,128]{1,3,2,0:T(8,128)(2,1)S(1)}, u32[]{:S(2)}, u32[]{:S(2)}) collective-permute-start(bf16[2,136,2,128]{1,3,2,0:T(8,128)(2,1)S(1)} %get-tuple-element.236), channel_id=1, source_target_pairs={{0,4},{4,8},{8,12},{12,0},{1,5},{5,9},{9,13},{13,1},{2,6},{6,10},{... | collective-permute-start | bytes 417800 | tf_op jit(solution)/shard_map/ppermute | solution.py:16
  51.4 9.2 %collective-permute-start.9 = (bf16[2,136,2,128]{1,3,2,0:T(8,128)(2,1)S(1)}, bf16[2,136,2,128]{1,3,2,0:T(8,128)(2,1)S(1)}, u32[]{:S(2)}, u32[]{:S(2)}) collective-permute-start(bf16[2,136,2,128]{1,3,2,0:T(8,128)(2,1)S(1)} %get-tuple-element.237), channel_id=1, source_target_pairs={{4,0},{8,4},{12,8},{0,12},{5,1},{9,5},{13,9},{1,13},{6,2},{10,6},{... | collective-permute-start | bytes 417800 | tf_op jit(solution)/shard_map/ppermute | solution.py:19
  60.6 3.9 %collective-permute-start.10 = (bf16[2,136,12,2]{1,3,2,0:T(2,128)(2,1)S(1)}, bf16[2,136,12,2]{1,3,2,0:T(2,128)(2,1)S(1)}, u32[]{:S(2)}, u32[]{:S(2)}) collective-permute-start(bf16[2,136,12,2]{1,3,2,0:T(2,128)(2,1)S(1)} %get-tuple-element.228), channel_id=1, source_target_pairs={{0,2},{2,0},{1,3},{3,1},{4,6},{6,4},{5,7},{7,5},{8,10},{10,8},{9,1... | collective-permute-start | bytes 39176 | tf_op jit(solution)/shard_map/ppermute | solution.py:16
  60.7 4.1 %collective-permute-start.11 = (bf16[2,136,12,2]{1,3,2,0:T(2,128)(2,1)S(1)}, bf16[2,136,12,2]{1,3,2,0:T(2,128)(2,1)S(1)}, u32[]{:S(2)}, u32[]{:S(2)}) collective-permute-start(bf16[2,136,12,2]{1,3,2,0:T(2,128)(2,1)S(1)} %get-tuple-element.229), channel_id=1, source_target_pairs={{2,0},{0,2},{3,1},{1,3},{6,4},{4,6},{7,5},{5,7},{10,8},{8,10},{11,... | collective-permute-start | bytes 39176 | tf_op jit(solution)/shard_map/ppermute | solution.py:19
  77.9 13.4 %collective-permute-start.12 = (bf16[2,136,4,128]{1,2,3,0:T(4,128)(2,1)}, bf16[2,136,4,128]{1,2,3,0:T(4,128)(2,1)S(1)}, u32[]{:S(2)}, u32[]{:S(2)}) collective-permute-start(bf16[2,136,4,128]{1,2,3,0:T(4,128)(2,1)} %get-tuple-element.234), channel_id=1, source_target_pairs={{0,4},{4,8},{8,12},{12,0},{1,5},{5,9},{9,13},{13,1},{2,6},{6,10},{... | collective-permute-start | bytes 835592 | tf_op jit(solution)/shard_map/ppermute | solution.py:16
  79.2 17.4 %collective-permute-start.13 = (bf16[2,136,4,128]{1,2,3,0:T(4,128)(2,1)S(1)}, bf16[2,136,4,128]{1,2,3,0:T(4,128)(2,1)S(1)}, u32[]{:S(2)}, u32[]{:S(2)}) collective-permute-start(bf16[2,136,4,128]{1,2,3,0:T(4,128)(2,1)S(1)} %get-tuple-element.235), channel_id=1, source_target_pairs={{4,0},{8,4},{12,8},{0,12},{5,1},{9,5},{13,9},{1,13},{6,2},{10,6},{... | collective-permute-start | bytes 835592 | tf_op jit(solution)/shard_map/ppermute | solution.py:19
  96.8 4.3 %collective-permute-start.14 = (bf16[2,136,16,4]{1,2,3,0:T(8,128)(2,1)S(1)}, bf16[2,136,16,4]{1,2,3,0:T(8,128)(2,1)S(1)}, u32[]{:S(2)}, u32[]{:S(2)}) collective-permute-start(bf16[2,136,16,4]{1,2,3,0:T(8,128)(2,1)S(1)} %get-tuple-element.224), channel_id=1, source_target_pairs={{0,2},{2,0},{1,3},{3,1},{4,6},{6,4},{5,7},{7,5},{8,10},{10,8},{9,1... | collective-permute-start | bytes 104456 | tf_op jit(solution)/shard_map/ppermute | solution.py:16
  96.8 5.0 %collective-permute-start.15 = (bf16[2,136,16,4]{1,2,3,0:T(8,128)(2,1)S(1)}, bf16[2,136,16,4]{1,2,3,0:T(8,128)(2,1)S(1)}, u32[]{:S(2)}, u32[]{:S(2)}) collective-permute-start(bf16[2,136,16,4]{1,2,3,0:T(8,128)(2,1)S(1)} %get-tuple-element.225), channel_id=1, source_target_pairs={{2,0},{0,2},{3,1},{1,3},{6,4},{4,6},{7,5},{5,7},{10,8},{8,10},{11,... | collective-permute-start | bytes 104456 | tf_op jit(solution)/shard_map/ppermute | solution.py:19
  124.8 5.6 %collective-permute-start.16 = (bf16[2,16,1,128]{3,2,1,0:T(2,128)(2,1)S(1)}, bf16[2,16,1,128]{3,2,1,0:T(2,128)(2,1)S(1)}, u32[]{:S(2)}, u32[]{:S(2)}) collective-permute-start(bf16[2,16,1,128]{3,2,1,0:T(2,128)(2,1)S(1)} %get-tuple-element.250), channel_id=1, source_target_pairs={{0,4},{4,8},{8,12},{12,0},{1,5},{5,9},{9,13},{13,1},{2,6},{6,10},{... | collective-permute-start | bytes 24584 | tf_op jit(solution)/shard_map/ppermute | solution.py:16
  125.1 5.2 %collective-permute-start.17 = (bf16[2,16,1,128]{3,2,1,0:T(2,128)(2,1)S(1)}, bf16[2,16,1,128]{3,2,1,0:T(2,128)(2,1)S(1)}, u32[]{:S(2)}, u32[]{:S(2)}) collective-permute-start(bf16[2,16,1,128]{3,2,1,0:T(2,128)(2,1)S(1)} %get-tuple-element.251), channel_id=1, source_target_pairs={{4,0},{8,4},{12,8},{0,12},{5,1},{9,5},{13,9},{1,13},{6,2},{10,6},{... | collective-permute-start | bytes 24584 | tf_op jit(solution)/shard_map/ppermute | solution.py:19
  132.3 6.3 %collective-permute-start.18 = (bf16[2,136,1,128]{3,1,2,0:T(8,128)(2,1)S(1)}, bf16[2,136,1,128]{3,1,2,0:T(8,128)(2,1)S(1)}, u32[]{:S(2)}, u32[]{:S(2)}) collective-permute-start(bf16[2,136,1,128]{3,1,2,0:T(8,128)(2,1)S(1)} %get-tuple-element.238), channel_id=1, source_target_pairs={{0,4},{4,8},{8,12},{12,0},{1,5},{5,9},{9,13},{13,1},{2,6},{6,10},{... | collective-permute-start | bytes 208904 | tf_op jit(solution)/shard_map/ppermute | solution.py:16
  132.4 6.3 %collective-permute-start.19 = (bf16[2,136,1,128]{3,1,2,0:T(8,128)(2,1)S(1)}, bf16[2,136,1,128]{3,1,2,0:T(8,128)(2,1)S(1)}, u32[]{:S(2)}, u32[]{:S(2)}) collective-permute-start(bf16[2,136,1,128]{3,1,2,0:T(8,128)(2,1)S(1)} %get-tuple-element.239), channel_id=1, source_target_pairs={{4,0},{8,4},{12,8},{0,12},{5,1},{9,5},{13,9},{1,13},{6,2},{10,6},{... | collective-permute-start | bytes 208904 | tf_op jit(solution)/shard_map/ppermute | solution.py:19
  156.6 5.8 %collective-permute-start.20 = (bf16[2,32,1,128]{3,2,1,0:T(2,128)(2,1)S(1)}, bf16[2,32,1,128]{3,2,1,0:T(2,128)(2,1)S(1)}, u32[]{:S(2)}, u32[]{:S(2)}) collective-permute-start(bf16[2,32,1,128]{3,2,1,0:T(2,128)(2,1)S(1)} %get-tuple-element.246), channel_id=1, source_target_pairs={{0,4},{4,8},{8,12},{12,0},{1,5},{5,9},{9,13},{13,1},{2,6},{6,10},{... | collective-permute-start | bytes 49160 | tf_op jit(solution)/shard_map/ppermute | solution.py:16
  157.9 4.5 %collective-permute-start.21 = (bf16[2,32,1,128]{3,2,1,0:T(2,128)(2,1)S(1)}, bf16[2,32,1,128]{3,2,1,0:T(2,128)(2,1)S(1)}, u32[]{:S(2)}, u32[]{:S(2)}) collective-permute-start(bf16[2,32,1,128]{3,2,1,0:T(2,128)(2,1)S(1)} %get-tuple-element.247), channel_id=1, source_target_pairs={{4,0},{8,4},{12,8},{0,12},{5,1},{9,5},{13,9},{1,13},{6,2},{10,6},{... | collective-permute-start | bytes 49160 | tf_op jit(solution)/shard_map/ppermute | solution.py:19
  162.7 6.4 %collective-permute-start.22 = (bf16[2,32,10,1]{3,2,1,0:T(8,128)(2,1)S(1)}, bf16[2,32,10,1]{3,2,1,0:T(8,128)(2,1)S(1)}, u32[]{:S(2)}, u32[]{:S(2)}) collective-permute-start(bf16[2,32,10,1]{3,2,1,0:T(8,128)(2,1)S(1)} %get-tuple-element.242), channel_id=1, source_target_pairs={{0,2},{2,0},{1,3},{3,1},{4,6},{6,4},{5,7},{7,5},{8,10},{10,8},{9,1... | collective-permute-start | bytes 3848 | tf_op jit(solution)/shard_map/ppermute | solution.py:16
  162.8 9.1 %collective-permute-start.23 = (bf16[2,32,10,1]{3,2,1,0:T(8,128)(2,1)S(1)}, bf16[2,32,10,1]{3,2,1,0:T(8,128)(2,1)S(1)}, u32[]{:S(2)}, u32[]{:S(2)}) collective-permute-start(bf16[2,32,10,1]{3,2,1,0:T(8,128)(2,1)S(1)} %get-tuple-element.243), channel_id=1, source_target_pairs={{2,0},{0,2},{3,1},{1,3},{6,4},{4,6},{7,5},{5,7},{10,8},{8,10},{11,... | collective-permute-start | bytes 3848 | tf_op jit(solution)/shard_map/ppermute | solution.py:19
  177.5 8.4 %collective-permute-start.24 = (bf16[2,136,2,128]{1,3,2,0:T(8,128)(2,1)S(1)}, bf16[2,136,2,128]{1,3,2,0:T(8,128)(2,1)S(1)}, u32[]{:S(2)}, u32[]{:S(2)}) collective-permute-start(bf16[2,136,2,128]{1,3,2,0:T(8,128)(2,1)S(1)} %get-tuple-element.232), channel_id=1, source_target_pairs={{0,4},{4,8},{8,12},{12,0},{1,5},{5,9},{9,13},{13,1},{2,6},{6,10},{... | collective-permute-start | bytes 417800 | tf_op jit(solution)/shard_map/ppermute | solution.py:16
  178.8 9.2 %collective-permute-start.25 = (bf16[2,136,2,128]{1,3,2,0:T(8,128)(2,1)S(1)}, bf16[2,136,2,128]{1,3,2,0:T(8,128)(2,1)S(1)}, u32[]{:S(2)}, u32[]{:S(2)}) collective-permute-start(bf16[2,136,2,128]{1,3,2,0:T(8,128)(2,1)S(1)} %get-tuple-element.233), channel_id=1, source_target_pairs={{4,0},{8,4},{12,8},{0,12},{5,1},{9,5},{13,9},{1,13},{6,2},{10,6},{... | collective-permute-start | bytes 417800 | tf_op jit(solution)/shard_map/ppermute | solution.py:19
  188.1 3.9 %collective-permute-start.26 = (bf16[2,136,12,2]{1,3,2,0:T(2,128)(2,1)S(1)}, bf16[2,136,12,2]{1,3,2,0:T(2,128)(2,1)S(1)}, u32[]{:S(2)}, u32[]{:S(2)}) collective-permute-start(bf16[2,136,12,2]{1,3,2,0:T(2,128)(2,1)S(1)} %get-tuple-element.226), channel_id=1, source_target_pairs={{0,2},{2,0},{1,3},{3,1},{4,6},{6,4},{5,7},{7,5},{8,10},{10,8},{9,1... | collective-permute-start | bytes 39176 | tf_op jit(solution)/shard_map/ppermute | solution.py:16
  188.1 4.1 %collective-permute-start.27 = (bf16[2,136,12,2]{1,3,2,0:T(2,128)(2,1)S(1)}, bf16[2,136,12,2]{1,3,2,0:T(2,128)(2,1)S(1)}, u32[]{:S(2)}, u32[]{:S(2)}) collective-permute-start(bf16[2,136,12,2]{1,3,2,0:T(2,128)(2,1)S(1)} %get-tuple-element.227), channel_id=1, source_target_pairs={{2,0},{0,2},{3,1},{1,3},{6,4},{4,6},{7,5},{5,7},{10,8},{8,10},{11,... | collective-permute-start | bytes 39176 | tf_op jit(solution)/shard_map/ppermute | solution.py:19
  206.5 11.1 %collective-permute-start.28 = (bf16[2,136,4,128]{1,2,3,0:T(4,128)(2,1)S(1)}, bf16[2,136,4,128]{1,2,3,0:T(4,128)(2,1)S(1)}, u32[]{:S(2)}, u32[]{:S(2)}) collective-permute-start(bf16[2,136,4,128]{1,2,3,0:T(4,128)(2,1)S(1)} %get-tuple-element.230), channel_id=1, source_target_pairs={{0,4},{4,8},{8,12},{12,0},{1,5},{5,9},{9,13},{13,1},{2,6},{6,10},{... | collective-permute-start | bytes 835592 | tf_op jit(solution)/shard_map/ppermute | solution.py:16
  207.7 14.8 %collective-permute-start.29 = (bf16[2,136,4,128]{1,2,3,0:T(4,128)(2,1)S(1)}, bf16[2,136,4,128]{1,2,3,0:T(4,128)(2,1)S(1)}, u32[]{:S(2)}, u32[]{:S(2)}) collective-permute-start(bf16[2,136,4,128]{1,2,3,0:T(4,128)(2,1)S(1)} %get-tuple-element.231), channel_id=1, source_target_pairs={{4,0},{8,4},{12,8},{0,12},{5,1},{9,5},{13,9},{1,13},{6,2},{10,6},{... | collective-permute-start | bytes 835592 | tf_op jit(solution)/shard_map/ppermute | solution.py:19
  222.5 4.3 %collective-permute-start.30 = (bf16[2,136,16,4]{1,2,3,0:T(8,128)(2,1)S(1)}, bf16[2,136,16,4]{1,2,3,0:T(8,128)(2,1)S(1)}, u32[]{:S(2)}, u32[]{:S(2)}) collective-permute-start(bf16[2,136,16,4]{1,2,3,0:T(8,128)(2,1)S(1)} %get-tuple-element.222), channel_id=1, source_target_pairs={{0,2},{2,0},{1,3},{3,1},{4,6},{6,4},{5,7},{7,5},{8,10},{10,8},{9,1... | collective-permute-start | bytes 104456 | tf_op jit(solution)/shard_map/ppermute | solution.py:16
  222.6 5.0 %collective-permute-start.31 = (bf16[2,136,16,4]{1,2,3,0:T(8,128)(2,1)S(1)}, bf16[2,136,16,4]{1,2,3,0:T(8,128)(2,1)S(1)}, u32[]{:S(2)}, u32[]{:S(2)}) collective-permute-start(bf16[2,136,16,4]{1,2,3,0:T(8,128)(2,1)S(1)} %get-tuple-element.223), channel_id=1, source_target_pairs={{2,0},{0,2},{3,1},{1,3},{6,4},{4,6},{7,5},{5,7},{10,8},{8,10},{11,... | collective-permute-start | bytes 104456 | tf_op jit(solution)/shard_map/ppermute | solution.py:19
  (23 other events, 129.4 us)
where the time goes:
time: 247 us; the launch traced here: 246 us
  waiting for transfers between devices  73.3 us (30%)
  starting transfers between devices  53.1 us (21%)
  local copies, waits for them, and re-layouts  46.3 us (19%)
  blocking collectives  38 us (15%)
  other arithmetic  22.2 us (9%)
  matrix products  10.6 us (4%)
    ppermute x16, waiting for transfers between devices, with_halo(): lax.ppermute(lax.slice_in_dim(block, block.shape[dim] - width, None, axis...  52.3 us
    ppermute x16, starting transfers between devices, with_halo(): lax.ppermute(lax.slice_in_dim(block, 0, width, axis=dim), axis, backward)  40.1 us
    psum x2, blocking collectives, spread_2(): return lax.psum(kept, axis)  33.4 us
    ppermute x16, waiting for transfers between devices, with_halo(): lax.ppermute(lax.slice_in_dim(block, 0, width, axis=dim), axis, backward)  20.9 us
    another operation x13, local copies, waits for them, and re-layouts  18.2 us
    cond x58, local copies, waits for them, and re-layouts  13.4 us
    ppermute x16, starting transfers between devices, with_halo(): lax.ppermute(lax.slice_in_dim(block, block.shape[dim] - width, None, axis...  13 us
    concatenate x12, other arithmetic, with_halo(): block = jnp.concatenate([low, block, high], axis=dim)  11.2 us
  transfers between devices with their start and end apart: 32, of which 27 were waited for; matrix products, arithmetic and copies ran while one was open for 0% of the time, Pallas kernels for 0%

commit v1 on v0

--- a/solution.py
+++ b/solution.py
@@ -23,7 +23,7 @@
 
 def spread_2(value, axis, source):
     kept = jnp.where(lax.axis_index(axis) == source, value, 0).astype(value.dtype)
-    return lax.psum(kept, axis)
+    return jnp.sum(lax.all_gather(kept, axis), axis=0)
 
 
 def tap_sum(source, weight, dilation):

time: 247 us -> 239 us (0.968)
  blocking collectives: 38 us -> 29.6 us
    psum x2 -> x0, blocking collectives: 33.4 us -> none  [spread_2(): return lax.psum(kept, axis)]
    all_gather x0 -> x2, blocking collectives: none -> 25 us  [spread_2(): return jnp.sum(lax.all_gather(kept, axis), axis=0)]
    ppermute x16, starting transfers between devices: 13 us -> 17.3 us  [with_halo(): lax.ppermute(lax.slice_in_dim(block, block.shape[dim] - width, None, axis...]
    ppermute x16, starting transfers between devices: 40.1 us -> 36.1 us  [with_halo(): lax.ppermute(lax.slice_in_dim(block, 0, width, axis=dim), axis, backward)]
where the time goes in v1:
time: 239 us; the launch traced here: 238 us
  waiting for transfers between devices  73.8 us (31%)
  starting transfers between devices  53.4 us (22%)
  local copies, waits for them, and re-layouts  46.3 us (19%)
  blocking collectives  29.6 us (12%)
  other arithmetic  22.2 us (9%)
  matrix products  10.6 us (4%)
    ppermute x16, waiting for transfers between devices, with_halo(): lax.ppermute(lax.slice_in_dim(block, block.shape[dim] - width, None, axis...  52.6 us
    ppermute x16, starting transfers between devices, with_halo(): lax.ppermute(lax.slice_in_dim(block, 0, width, axis=dim), axis, backward)  36.1 us
    all_gather x2, blocking collectives, spread_2(): return jnp.sum(lax.all_gather(kept, axis), axis=0)  25 us
    ppermute x16, waiting for transfers between devices, with_halo(): lax.ppermute(lax.slice_in_dim(block, 0, width, axis=dim), axis, backward)  21.2 us
    another operation x13, local copies, waits for them, and re-layouts  18.2 us
    ppermute x16, starting transfers between devices, with_halo(): lax.ppermute(lax.slice_in_dim(block, block.shape[dim] - width, None, axis...  17.3 us
    cond x58, local copies, waits for them, and re-layouts  13.4 us
    concatenate x12, other arithmetic, with_halo(): block = jnp.concatenate([low, block, high], axis=dim)  11.2 us
  transfers between devices with their start and end apart: 32, of which 27 were waited for; matrix products, arithmetic and copies ran while one was open for 0% of the time, Pallas kernels for 0%

profile of v1, /device:TPU:0, one launch (start us, length us, event | category | flops | bytes accessed | tf_op | source)
XLA Modules:
  0.0 238.0 jit_solution(12883848074267271107)
XLA Ops:
  2.2 3.1 %collective-permute-start = (bf16[2,16,1,128]{3,1,2,0:T(8,128)(2,1)S(1)}, bf16[2,16,1,128]{3,1,2,0:T(8,128)(2,1)S(1)}, u32[]{:S(2)}, u32[]{:S(2)}) collective-permute-start(bf16[2,16,1,128]{3,1,2,0:T(8,128)(2,1)S(1)} %get-tuple-element.252), channel_id=1, source_target_pairs={{0,4},{4,8},{8,12},{12,0},{1,5},{5,9},{9,13},{13,1},{2,6},{6,10},{... | collective-permute-start | bytes 24584 | tf_op jit(solution)/shard_map/ppermute | solution.py:16
  16.7 13.2 %all-gather = bf16[4,8,8,128]{3,2,1,0:T(8,128)(2,1)S(1)} all-gather(bf16[2,8,8,128]{3,2,1,0:T(8,128)(2,1)S(1)} %fusion.76), channel_id=2, replica_groups=mesh['grp'=2,'sp'=4,'sec'=2,'mb'=2] {'sec'}, dimensions={0}, use_global_device_ids=true | all-gather | bytes 98304 | tf_op jit(solution)/shard_map/all_gather | solution.py:26
  31.0 2.8 %collective-permute-start.5 = (bf16[2,32,1,128]{3,1,2,0:T(8,128)(2,1)S(1)}, bf16[2,32,1,128]{3,1,2,0:T(8,128)(2,1)S(1)}, u32[]{:S(2)}, u32[]{:S(2)}) collective-permute-start(bf16[2,32,1,128]{3,1,2,0:T(8,128)(2,1)S(1)} %get-tuple-element.249), channel_id=1, source_target_pairs={{4,0},{8,4},{12,8},{0,12},{5,1},{9,5},{13,9},{1,13},{6,2},{10,6},{... | collective-permute-start | bytes 49160 | tf_op jit(solution)/shard_map/ppermute | solution.py:19
  38.4 2.7 %collective-permute-done.6 = bf16[2,32,10,1]{3,1,2,0:T(8,128)(2,1)S(1)} collective-permute-done((bf16[2,32,10,1]{3,1,2,0:T(8,128)(2,1)S(1)}, bf16[2,32,10,1]{3,1,2,0:T(8,128)(2,1)S(1)}, u32[]{:S(2)}, u32[]{:S(2)}) %collective-permute-start.6) | collective-permute-done | bytes 1312 | tf_op jit(solution)/shard_map/ppermute | solution.py:16
  47.3 2.8 %collective-permute-start.9 = (bf16[2,136,2,128]{1,3,2,0:T(8,128)(2,1)S(1)}, bf16[2,136,2,128]{1,3,2,0:T(8,128)(2,1)S(1)}, u32[]{:S(2)}, u32[]{:S(2)}) collective-permute-start(bf16[2,136,2,128]{1,3,2,0:T(8,128)(2,1)S(1)} %get-tuple-element.237), channel_id=1, source_target_pairs={{4,0},{8,4},{12,8},{0,12},{5,1},{9,5},{13,9},{1,13},{6,2},{10,6},{... | collective-permute-start | bytes 417800 | tf_op jit(solution)/shard_map/ppermute | solution.py:19
  50.2 4.4 %collective-permute-done.8 = bf16[2,136,2,128]{1,3,2,0:T(8,128)(2,1)S(1)} collective-permute-done((bf16[2,136,2,128]{1,3,2,0:T(8,128)(2,1)S(1)}, bf16[2,136,2,128]{1,3,2,0:T(8,128)(2,1)S(1)}, u32[]{:S(2)}, u32[]{:S(2)}) %collective-permute-start.8) | collective-permute-done | bytes 139296 | tf_op jit(solution)/shard_map/ppermute | solution.py:16
  63.8 8.1 %conditional.13 = (bf16[2,136,8,128]{3,1,2,0:T(8,128)(2,1)S(1)}) conditional(s32[]{:T(128)} %convert_element_type.72, (pred[132]{0:T(512)(128)(4,1)S(1)}, bf16[2,136,12,132]{1,3,2,0:T(8,128)(2,1)S(1)}, bf16[2,136,12,132]{3,1,2,0:T(8,128)(2,1)}, bf16[3,3,136,136]{3,2,1,0:T(8,128)(2,1)}) %tuple.76, () %tuple.77), branch_computations={%region_7.8_spmd, %region_8.9_spmd} | conditional | flops 684774144 | bytes 21570856 | solution.py:142
  77.7 10.0 %collective-permute-done.12 = bf16[2,136,4,128]{1,2,3,0:T(4,128)(2,1)S(1)} collective-permute-done((bf16[2,136,4,128]{1,2,3,0:T(4,128)(2,1)}, bf16[2,136,4,128]{1,2,3,0:T(4,128)(2,1)S(1)}, u32[]{:S(2)}, u32[]{:S(2)}) %collective-permute-start.12) | collective-permute-done | bytes 278560 | tf_op jit(solution)/shard_map/ppermute | solution.py:16
  87.8 5.3 %collective-permute-done.13 = bf16[2,136,4,128]{1,2,3,0:T(4,128)(2,1)S(1)} collective-permute-done((bf16[2,136,4,128]{1,2,3,0:T(4,128)(2,1)S(1)}, bf16[2,136,4,128]{1,2,3,0:T(4,128)(2,1)S(1)}, u32[]{:S(2)}, u32[]{:S(2)}) %collective-permute-start.13) | collective-permute-done | bytes 278560 | tf_op jit(solution)/shard_map/ppermute | solution.py:19
  98.2 2.6 %pad_maximum_fusion = bf16[2,136,16,136]{1,2,3,0:T(8,128)(2,1)} fusion(bf16[2,136,16,4]{1,2,3,0:T(8,128)(2,1)S(1)} %collective-permute-done.15, bf16[2,136,4,128]{1,2,3,0:T(4,128)(2,1)S(1)} %collective-permute-done.13, bf16[2,136,8,128]{1,2,3,0:T(8,128)(2,1)S(1)} %copy.69, bf16[2,136,4,128]{1,2,3,0:T(4,128)(2,1)S(1)} %collective-permute-done.12, ...), kind=kLoop, calls=%fused_computation.188 | loop fusion | flops 5918720 | bytes 2367488 | tf_op jit(solution)/shard_map/concatenate | solution.py:20
  101.8 14.8 %conditional.14 = (f32[2,32,8,128]{3,2,1,0:T(8,128)S(1)}, f32[2,24,8,128]{3,2,1,0:T(8,128)S(1)}) conditional(s32[]{:T(128)} %convert_element_type.72, (pred[136]{0:T(512)(128)(4,1)S(1)}, bf16[2,136,16,136]{1,2,3,0:T(8,128)(2,1)}, bf16[2,136,16,136]{3,1,2,0:T(8,128)(2,1)S(1)}, bf16[3,3,136,32]{2,3,1,0:T(8,128)(2,1)S(1)}) %tuple.159, () %tuple.79), branch_computations={%region_9.10_spmd, %region_10.11_spmd} | conditional | flops 161024000 | bytes 42584756 | solution.py:142
  101.8 4.6 %copy.72 = bf16[2,136,16,136]{3,1,2,0:T(8,128)(2,1)} copy(bf16[2,136,16,136]{1,2,3,0:T(8,128)(2,1)} %get-tuple-element.198) | data formatting | bytes 2367488 | tf_op jit(solution)/shard_map
  113.0 3.3 %convolution_bitcast_fusion.4 = f32[2,32,8,128]{3,1,2,0:T(8,128)S(1)} fusion(bf16[2,1224,8,128]{3,1,2,0:T(8,128)(2,1)} %copy-done.2, bf16[1224,32,1,1]{0,1,2,3:T(8,128)(2,1)S(1)} %reshape.62), kind=kOutput, calls=%fused_computation.83 | convolution fusion | flops 160432128 | bytes 5353984 | tf_op jit(solution)/shard_map/cond/branch_0_fun/mkrc,ko->morc/dot_general | solution.py:44
  116.6 4.6 %all_gather.17 = bf16[2,8,8,256]{3,2,1,0:T(8,128)(2,1)S(1)} all-gather(bf16[2,8,8,128]{3,2,1,0:T(8,128)(2,1)S(1)} %slice.832), channel_id=1, replica_groups=mesh['grp'=2,'sp'=4,'sec'=2,'mb'=2] {'sec'}, dimensions={3}, use_global_device_ids=true | all-gather | bytes 98304 | tf_op jit(solution)/shard_map/all_gather | solution.py:172
  121.6 3.5 %collective-permute-start.17 = (bf16[2,16,1,128]{3,2,1,0:T(2,128)(2,1)S(1)}, bf16[2,16,1,128]{3,2,1,0:T(2,128)(2,1)S(1)}, u32[]{:S(2)}, u32[]{:S(2)}) collective-permute-start(bf16[2,16,1,128]{3,2,1,0:T(2,128)(2,1)S(1)} %get-tuple-element.251), channel_id=1, source_target_pairs={{4,0},{8,4},{12,8},{0,12},{5,1},{9,5},{13,9},{1,13},{6,2},{10,6},{... | collective-permute-start | bytes 24584 | tf_op jit(solution)/shard_map/ppermute | solution.py:19
  128.8 3.9 %collective-permute-start.19 = (bf16[2,136,1,128]{3,1,2,0:T(8,128)(2,1)S(1)}, bf16[2,136,1,128]{3,1,2,0:T(8,128)(2,1)S(1)}, u32[]{:S(2)}, u32[]{:S(2)}) collective-permute-start(bf16[2,136,1,128]{3,1,2,0:T(8,128)(2,1)S(1)} %get-tuple-element.239), channel_id=1, source_target_pairs={{4,0},{8,4},{12,8},{0,12},{5,1},{9,5},{13,9},{1,13},{6,2},{10,6},{... | collective-permute-start | bytes 208904 | tf_op jit(solution)/shard_map/ppermute | solution.py:19
  136.8 11.8 %all-gather.1 = bf16[4,8,8,128]{3,2,1,0:T(8,128)(2,1)S(1)} all-gather(bf16[2,8,8,128]{3,2,1,0:T(8,128)(2,1)S(1)} %fusion.77), channel_id=3, replica_groups=mesh['grp'=2,'sp'=4,'sec'=2,'mb'=2] {'sec'}, dimensions={0}, use_global_device_ids=true | all-gather | bytes 98304 | tf_op jit(solution)/shard_map/all_gather | solution.py:26
  150.4 2.6 %collective-permute-start.21 = (bf16[2,32,1,128]{3,2,1,0:T(2,128)(2,1)S(1)}, bf16[2,32,1,128]{3,2,1,0:T(2,128)(2,1)S(1)}, u32[]{:S(2)}, u32[]{:S(2)}) collective-permute-start(bf16[2,32,1,128]{3,2,1,0:T(2,128)(2,1)S(1)} %get-tuple-element.247), channel_id=1, source_target_pairs={{4,0},{8,4},{12,8},{0,12},{5,1},{9,5},{13,9},{1,13},{6,2},{10,6},{... | collective-permute-start | bytes 49160 | tf_op jit(solution)/shard_map/ppermute | solution.py:19
  157.3 4.3 %collective-permute-done.22 = bf16[2,32,10,1]{3,2,1,0:T(8,128)(2,1)S(1)} collective-permute-done((bf16[2,32,10,1]{3,2,1,0:T(8,128)(2,1)S(1)}, bf16[2,32,10,1]{3,2,1,0:T(8,128)(2,1)S(1)}, u32[]{:S(2)}, u32[]{:S(2)}) %collective-permute-start.22) | collective-permute-done | bytes 1312 | tf_op jit(solution)/shard_map/ppermute | solution.py:16
  161.6 2.8 %collective-permute-done.23 = bf16[2,32,10,1]{3,2,1,0:T(8,128)(2,1)S(1)} collective-permute-done((bf16[2,32,10,1]{3,2,1,0:T(8,128)(2,1)S(1)}, bf16[2,32,10,1]{3,2,1,0:T(8,128)(2,1)S(1)}, u32[]{:S(2)}, u32[]{:S(2)}) %collective-permute-start.23) | collective-permute-done | bytes 1312 | tf_op jit(solution)/shard_map/ppermute | solution.py:19
  165.0 2.7 %conditional.17 = (bf16[2,136,8,128]{3,1,2,0:T(8,128)(2,1)S(1)}) conditional(s32[]{:T(128)} %convert_element_type.72, (pred[130]{0:T(512)(128)(4,1)}, bf16[2,32,10,130]{3,2,1,0:T(8,128)(2,1)S(1)}, bf16[2,32,10,130]{3,1,2,0:T(8,128)(2,1)S(1)}, bf16[3,3,32,136]{3,2,1,0:T(8,128)(2,1)}) %tuple.84, () %tuple.85), branch_computations={%region_16.17_spmd, %region_17.18_spmd} | conditional | flops 163022080 | bytes 4987046 | solution.py:142
  171.3 2.7 %collective-permute-start.25 = (bf16[2,136,2,128]{1,3,2,0:T(8,128)(2,1)S(1)}, bf16[2,136,2,128]{1,3,2,0:T(8,128)(2,1)S(1)}, u32[]{:S(2)}, u32[]{:S(2)}) collective-permute-start(bf16[2,136,2,128]{1,3,2,0:T(8,128)(2,1)S(1)} %get-tuple-element.233), channel_id=1, source_target_pairs={{4,0},{8,4},{12,8},{0,12},{5,1},{9,5},{13,9},{1,13},{6,2},{10,6},{... | collective-permute-start | bytes 417800 | tf_op jit(solution)/shard_map/ppermute | solution.py:19
  174.0 4.4 %collective-permute-done.24 = bf16[2,136,2,128]{1,3,2,0:T(8,128)(2,1)S(1)} collective-permute-done((bf16[2,136,2,128]{1,3,2,0:T(8,128)(2,1)S(1)}, bf16[2,136,2,128]{1,3,2,0:T(8,128)(2,1)S(1)}, u32[]{:S(2)}, u32[]{:S(2)}) %collective-permute-start.24) | collective-permute-done | bytes 139296 | tf_op jit(solution)/shard_map/ppermute | solution.py:16
  186.6 9.4 %conditional.18 = (bf16[2,136,8,128]{3,1,2,0:T(8,128)(2,1)S(1)}) conditional(s32[]{:T(128)} %convert_element_type.72, (pred[132]{0:T(512)(128)(4,1)S(1)}, bf16[2,136,12,132]{1,3,2,0:T(8,128)(2,1)}, bf16[2,136,12,132]{3,1,2,0:T(8,128)(2,1)}, bf16[3,3,136,136]{3,2,1,0:T(8,128)(2,1)}) %tuple.164, () %tuple.87), branch_computations={%region_18.19_spmd, %region_19.20_spmd} | conditional | flops 684774144 | bytes 21570856 | solution.py:142
  186.6 3.8 %copy.83 = bf16[2,136,12,132]{3,1,2,0:T(8,128)(2,1)} copy(bf16[2,136,12,132]{1,3,2,0:T(8,128)(2,1)} %get-tuple-element.210) | data formatting | bytes 1723392 | tf_op jit(solution)/shard_map
  200.2 2.7 %collective-permute-start.29 = (bf16[2,136,4,128]{1,2,3,0:T(4,128)(2,1)S(1)}, bf16[2,136,4,128]{1,2,3,0:T(4,128)(2,1)S(1)}, u32[]{:S(2)}, u32[]{:S(2)}) collective-permute-start(bf16[2,136,4,128]{1,2,3,0:T(4,128)(2,1)S(1)} %get-tuple-element.231), channel_id=1, source_target_pairs={{4,0},{8,4},{12,8},{0,12},{5,1},{9,5},{13,9},{1,13},{6,2},{10,6},{... | collective-permute-start | bytes 835592 | tf_op jit(solution)/shard_map/ppermute | solution.py:19
  202.8 7.3 %collective-permute-done.28 = bf16[2,136,4,128]{1,2,3,0:T(4,128)(2,1)S(1)} collective-permute-done((bf16[2,136,4,128]{1,2,3,0:T(4,128)(2,1)S(1)}, bf16[2,136,4,128]{1,2,3,0:T(4,128)(2,1)S(1)}, u32[]{:S(2)}, u32[]{:S(2)}) %collective-permute-start.28) | collective-permute-done | bytes 278560 | tf_op jit(solution)/shard_map/ppermute | solution.py:16
  210.1 4.9 %collective-permute-done.29 = bf16[2,136,4,128]{1,2,3,0:T(4,128)(2,1)S(1)} collective-permute-done((bf16[2,136,4,128]{1,2,3,0:T(4,128)(2,1)S(1)}, bf16[2,136,4,128]{1,2,3,0:T(4,128)(2,1)S(1)}, u32[]{:S(2)}, u32[]{:S(2)}) %collective-permute-start.29) | collective-permute-done | bytes 278560 | tf_op jit(solution)/shard_map/ppermute | solution.py:19
  220.1 2.6 %pad_maximum_fusion.1 = bf16[2,136,16,136]{1,2,3,0:T(8,128)(2,1)} fusion(bf16[2,136,16,4]{1,2,3,0:T(8,128)(2,1)S(1)} %collective-permute-done.31, bf16[2,136,4,128]{1,2,3,0:T(4,128)(2,1)S(1)} %collective-permute-done.29, bf16[2,136,8,128]{1,2,3,0:T(8,128)(2,1)S(1)} %copy.84, bf16[2,136,4,128]{1,2,3,0:T(4,128)(2,1)S(1)} %collective-permute-done.28, ...), kind=kLoop, calls=%fused_computation.189 | loop fusion | flops 5918720 | bytes 2367488 | tf_op jit(solution)/shard_map/concatenate | solution.py:20
  222.7 14.7 %conditional.19 = (f32[2,24,8,128]{3,2,1,0:T(8,128)S(1)}) conditional(s32[]{:T(128)} %convert_element_type.72, (pred[136]{0:T(512)(128)(4,1)S(1)}, bf16[2,136,16,136]{1,2,3,0:T(8,128)(2,1)}, bf16[2,136,16,136]{3,1,2,0:T(8,128)(2,1)S(1)}, bf16[3,3,136,32]{2,3,1,0:T(8,128)(2,1)S(1)}) %tuple.163, () %tuple.89), branch_computations={%region_20.21_spmd, %region_21.22_spmd} | conditional | flops 161024000 | bytes 42453676 | solution.py:142
  222.7 4.6 %copy.87 = bf16[2,136,16,136]{3,1,2,0:T(8,128)(2,1)} copy(bf16[2,136,16,136]{1,2,3,0:T(8,128)(2,1)} %get-tuple-element.214) | data formatting | bytes 2367488 | tf_op jit(solution)/shard_map
  233.9 3.3 %convolution_bitcast_fusion.9 = f32[2,32,8,128]{3,1,2,0:T(8,128)S(1)} fusion(bf16[2,1224,8,128]{3,1,2,0:T(8,128)(2,1)} %copy-done.3, bf16[1224,32,1,1]{0,1,2,3:T(8,128)(2,1)S(1)} %reshape.67), kind=kOutput, calls=%fused_computation.177 | convolution fusion | flops 160432128 | bytes 5353984 | tf_op jit(solution)/shard_map/cond/branch_0_fun/mkrc,ko->morc/dot_general | solution.py:44
  (226 shorter events, 114.6 us)
Async XLA Ops:
  2.2 6.8 %collective-permute-start = (bf16[2,16,1,128]{3,1,2,0:T(8,128)(2,1)S(1)}, bf16[2,16,1,128]{3,1,2,0:T(8,128)(2,1)S(1)}, u32[]{:S(2)}, u32[]{:S(2)}) collective-permute-start(bf16[2,16,1,128]{3,1,2,0:T(8,128)(2,1)S(1)} %get-tuple-element.252), channel_id=1, source_target_pairs={{0,4},{4,8},{8,12},{12,0},{1,5},{5,9},{9,13},{13,1},{2,6},{6,10},{... | collective-permute-start | bytes 24584 | tf_op jit(solution)/shard_map/ppermute | solution.py:16
  5.3 3.7 %collective-permute-start.1 = (bf16[2,16,1,128]{3,1,2,0:T(8,128)(2,1)S(1)}, bf16[2,16,1,128]{3,1,2,0:T(8,128)(2,1)S(1)}, u32[]{:S(2)}, u32[]{:S(2)}) collective-permute-start(bf16[2,16,1,128]{3,1,2,0:T(8,128)(2,1)S(1)} %get-tuple-element.253), channel_id=1, source_target_pairs={{4,0},{8,4},{12,8},{0,12},{5,1},{9,5},{13,9},{1,13},{6,2},{10,6},{... | collective-permute-start | bytes 24584 | tf_op jit(solution)/shard_map/ppermute | solution.py:19
  9.2 6.4 %collective-permute-start.2 = (bf16[2,136,1,128]{3,1,2,0:T(8,128)(2,1)S(1)}, bf16[2,136,1,128]{3,1,2,0:T(8,128)(2,1)S(1)}, u32[]{:S(2)}, u32[]{:S(2)}) collective-permute-start(bf16[2,136,1,128]{3,1,2,0:T(8,128)(2,1)S(1)} %get-tuple-element.240), channel_id=1, source_target_pairs={{0,4},{4,8},{8,12},{12,0},{1,5},{5,9},{9,13},{13,1},{2,6},{6,10},{... | collective-permute-start | bytes 208904 | tf_op jit(solution)/shard_map/ppermute | solution.py:16
  10.7 5.1 %collective-permute-start.3 = (bf16[2,136,1,128]{3,1,2,0:T(8,128)(2,1)S(1)}, bf16[2,136,1,128]{3,1,2,0:T(8,128)(2,1)S(1)}, u32[]{:S(2)}, u32[]{:S(2)}) collective-permute-start(bf16[2,136,1,128]{3,1,2,0:T(8,128)(2,1)S(1)} %get-tuple-element.241), channel_id=1, source_target_pairs={{4,0},{8,4},{12,8},{0,12},{5,1},{9,5},{13,9},{1,13},{6,2},{10,6},{... | collective-permute-start | bytes 208904 | tf_op jit(solution)/shard_map/ppermute | solution.py:19
  29.9 5.6 %collective-permute-start.4 = (bf16[2,32,1,128]{3,1,2,0:T(8,128)(2,1)S(1)}, bf16[2,32,1,128]{3,1,2,0:T(8,128)(2,1)S(1)}, u32[]{:S(2)}, u32[]{:S(2)}) collective-permute-start(bf16[2,32,1,128]{3,1,2,0:T(8,128)(2,1)S(1)} %get-tuple-element.248), channel_id=1, source_target_pairs={{0,4},{4,8},{8,12},{12,0},{1,5},{5,9},{9,13},{13,1},{2,6},{6,10},{... | collective-permute-start | bytes 49160 | tf_op jit(solution)/shard_map/ppermute | solution.py:16
  31.0 4.5 %collective-permute-start.5 = (bf16[2,32,1,128]{3,1,2,0:T(8,128)(2,1)S(1)}, bf16[2,32,1,128]{3,1,2,0:T(8,128)(2,1)S(1)}, u32[]{:S(2)}, u32[]{:S(2)}) collective-permute-start(bf16[2,32,1,128]{3,1,2,0:T(8,128)(2,1)S(1)} %get-tuple-element.249), channel_id=1, source_target_pairs={{4,0},{8,4},{12,8},{0,12},{5,1},{9,5},{13,9},{1,13},{6,2},{10,6},{... | collective-permute-start | bytes 49160 | tf_op jit(solution)/shard_map/ppermute | solution.py:19
  35.7 5.4 %collective-permute-start.6 = (bf16[2,32,10,1]{3,1,2,0:T(8,128)(2,1)S(1)}, bf16[2,32,10,1]{3,1,2,0:T(8,128)(2,1)S(1)}, u32[]{:S(2)}, u32[]{:S(2)}) collective-permute-start(bf16[2,32,10,1]{3,1,2,0:T(8,128)(2,1)S(1)} %get-tuple-element.244), channel_id=1, source_target_pairs={{0,2},{2,0},{1,3},{3,1},{4,6},{6,4},{5,7},{7,5},{8,10},{10,8},{9,1... | collective-permute-start | bytes 3848 | tf_op jit(solution)/shard_map/ppermute | solution.py:16
  37.8 5.3 %collective-permute-start.7 = (bf16[2,32,10,1]{3,1,2,0:T(8,128)(2,1)S(1)}, bf16[2,32,10,1]{3,1,2,0:T(8,128)(2,1)S(1)}, u32[]{:S(2)}, u32[]{:S(2)}) collective-permute-start(bf16[2,32,10,1]{3,1,2,0:T(8,128)(2,1)S(1)} %get-tuple-element.245), channel_id=1, source_target_pairs={{2,0},{0,2},{3,1},{1,3},{6,4},{4,6},{7,5},{5,7},{10,8},{8,10},{11,... | collective-permute-start | bytes 3848 | tf_op jit(solution)/shard_map/ppermute | solution.py:19
  46.2 8.3 %collective-permute-start.8 = (bf16[2,136,2,128]{1,3,2,0:T(8,128)(2,1)S(1)}, bf16[2,136,2,128]{1,3,2,0:T(8,128)(2,1)S(1)}, u32[]{:S(2)}, u32[]{:S(2)}) collective-permute-start(bf16[2,136,2,128]{1,3,2,0:T(8,128)(2,1)S(1)} %get-tuple-element.236), channel_id=1, source_target_pairs={{0,4},{4,8},{8,12},{12,0},{1,5},{5,9},{9,13},{13,1},{2,6},{6,10},{... | collective-permute-start | bytes 417800 | tf_op jit(solution)/shard_map/ppermute | solution.py:16
  47.3 9.2 %collective-permute-start.9 = (bf16[2,136,2,128]{1,3,2,0:T(8,128)(2,1)S(1)}, bf16[2,136,2,128]{1,3,2,0:T(8,128)(2,1)S(1)}, u32[]{:S(2)}, u32[]{:S(2)}) collective-permute-start(bf16[2,136,2,128]{1,3,2,0:T(8,128)(2,1)S(1)} %get-tuple-element.237), channel_id=1, source_target_pairs={{4,0},{8,4},{12,8},{0,12},{5,1},{9,5},{13,9},{1,13},{6,2},{10,6},{... | collective-permute-start | bytes 417800 | tf_op jit(solution)/shard_map/ppermute | solution.py:19
  56.6 3.9 %collective-permute-start.10 = (bf16[2,136,12,2]{1,3,2,0:T(2,128)(2,1)S(1)}, bf16[2,136,12,2]{1,3,2,0:T(2,128)(2,1)S(1)}, u32[]{:S(2)}, u32[]{:S(2)}) collective-permute-start(bf16[2,136,12,2]{1,3,2,0:T(2,128)(2,1)S(1)} %get-tuple-element.228), channel_id=1, source_target_pairs={{0,2},{2,0},{1,3},{3,1},{4,6},{6,4},{5,7},{7,5},{8,10},{10,8},{9,1... | collective-permute-start | bytes 39176 | tf_op jit(solution)/shard_map/ppermute | solution.py:16
  56.7 4.1 %collective-permute-start.11 = (bf16[2,136,12,2]{1,3,2,0:T(2,128)(2,1)S(1)}, bf16[2,136,12,2]{1,3,2,0:T(2,128)(2,1)S(1)}, u32[]{:S(2)}, u32[]{:S(2)}) collective-permute-start(bf16[2,136,12,2]{1,3,2,0:T(2,128)(2,1)S(1)} %get-tuple-element.229), channel_id=1, source_target_pairs={{2,0},{0,2},{3,1},{1,3},{6,4},{4,6},{7,5},{5,7},{10,8},{8,10},{11,... | collective-permute-start | bytes 39176 | tf_op jit(solution)/shard_map/ppermute | solution.py:19
  73.9 13.9 %collective-permute-start.12 = (bf16[2,136,4,128]{1,2,3,0:T(4,128)(2,1)}, bf16[2,136,4,128]{1,2,3,0:T(4,128)(2,1)S(1)}, u32[]{:S(2)}, u32[]{:S(2)}) collective-permute-start(bf16[2,136,4,128]{1,2,3,0:T(4,128)(2,1)} %get-tuple-element.234), channel_id=1, source_target_pairs={{0,4},{4,8},{8,12},{12,0},{1,5},{5,9},{9,13},{13,1},{2,6},{6,10},{... | collective-permute-start | bytes 835592 | tf_op jit(solution)/shard_map/ppermute | solution.py:16
  75.2 17.9 %collective-permute-start.13 = (bf16[2,136,4,128]{1,2,3,0:T(4,128)(2,1)S(1)}, bf16[2,136,4,128]{1,2,3,0:T(4,128)(2,1)S(1)}, u32[]{:S(2)}, u32[]{:S(2)}) collective-permute-start(bf16[2,136,4,128]{1,2,3,0:T(4,128)(2,1)S(1)} %get-tuple-element.235), channel_id=1, source_target_pairs={{4,0},{8,4},{12,8},{0,12},{5,1},{9,5},{13,9},{1,13},{6,2},{10,6},{... | collective-permute-start | bytes 835592 | tf_op jit(solution)/shard_map/ppermute | solution.py:19
  93.2 4.3 %collective-permute-start.14 = (bf16[2,136,16,4]{1,2,3,0:T(8,128)(2,1)S(1)}, bf16[2,136,16,4]{1,2,3,0:T(8,128)(2,1)S(1)}, u32[]{:S(2)}, u32[]{:S(2)}) collective-permute-start(bf16[2,136,16,4]{1,2,3,0:T(8,128)(2,1)S(1)} %get-tuple-element.224), channel_id=1, source_target_pairs={{0,2},{2,0},{1,3},{3,1},{4,6},{6,4},{5,7},{7,5},{8,10},{10,8},{9,1... | collective-permute-start | bytes 104456 | tf_op jit(solution)/shard_map/ppermute | solution.py:16
  93.3 5.0 %collective-permute-start.15 = (bf16[2,136,16,4]{1,2,3,0:T(8,128)(2,1)S(1)}, bf16[2,136,16,4]{1,2,3,0:T(8,128)(2,1)S(1)}, u32[]{:S(2)}, u32[]{:S(2)}) collective-permute-start(bf16[2,136,16,4]{1,2,3,0:T(8,128)(2,1)S(1)} %get-tuple-element.225), channel_id=1, source_target_pairs={{2,0},{0,2},{3,1},{1,3},{6,4},{4,6},{7,5},{5,7},{10,8},{8,10},{11,... | collective-permute-start | bytes 104456 | tf_op jit(solution)/shard_map/ppermute | solution.py:19
  121.2 5.6 %collective-permute-start.16 = (bf16[2,16,1,128]{3,2,1,0:T(2,128)(2,1)S(1)}, bf16[2,16,1,128]{3,2,1,0:T(2,128)(2,1)S(1)}, u32[]{:S(2)}, u32[]{:S(2)}) collective-permute-start(bf16[2,16,1,128]{3,2,1,0:T(2,128)(2,1)S(1)} %get-tuple-element.250), channel_id=1, source_target_pairs={{0,4},{4,8},{8,12},{12,0},{1,5},{5,9},{9,13},{13,1},{2,6},{6,10},{... | collective-permute-start | bytes 24584 | tf_op jit(solution)/shard_map/ppermute | solution.py:16
  121.6 5.2 %collective-permute-start.17 = (bf16[2,16,1,128]{3,2,1,0:T(2,128)(2,1)S(1)}, bf16[2,16,1,128]{3,2,1,0:T(2,128)(2,1)S(1)}, u32[]{:S(2)}, u32[]{:S(2)}) collective-permute-start(bf16[2,16,1,128]{3,2,1,0:T(2,128)(2,1)S(1)} %get-tuple-element.251), channel_id=1, source_target_pairs={{4,0},{8,4},{12,8},{0,12},{5,1},{9,5},{13,9},{1,13},{6,2},{10,6},{... | collective-permute-start | bytes 24584 | tf_op jit(solution)/shard_map/ppermute | solution.py:19
  128.7 6.2 %collective-permute-start.18 = (bf16[2,136,1,128]{3,1,2,0:T(8,128)(2,1)S(1)}, bf16[2,136,1,128]{3,1,2,0:T(8,128)(2,1)S(1)}, u32[]{:S(2)}, u32[]{:S(2)}) collective-permute-start(bf16[2,136,1,128]{3,1,2,0:T(8,128)(2,1)S(1)} %get-tuple-element.238), channel_id=1, source_target_pairs={{0,4},{4,8},{8,12},{12,0},{1,5},{5,9},{9,13},{13,1},{2,6},{6,10},{... | collective-permute-start | bytes 208904 | tf_op jit(solution)/shard_map/ppermute | solution.py:16
  128.8 6.1 %collective-permute-start.19 = (bf16[2,136,1,128]{3,1,2,0:T(8,128)(2,1)S(1)}, bf16[2,136,1,128]{3,1,2,0:T(8,128)(2,1)S(1)}, u32[]{:S(2)}, u32[]{:S(2)}) collective-permute-start(bf16[2,136,1,128]{3,1,2,0:T(8,128)(2,1)S(1)} %get-tuple-element.239), channel_id=1, source_target_pairs={{4,0},{8,4},{12,8},{0,12},{5,1},{9,5},{13,9},{1,13},{6,2},{10,6},{... | collective-permute-start | bytes 208904 | tf_op jit(solution)/shard_map/ppermute | solution.py:19
  148.7 6.1 %collective-permute-start.20 = (bf16[2,32,1,128]{3,2,1,0:T(2,128)(2,1)S(1)}, bf16[2,32,1,128]{3,2,1,0:T(2,128)(2,1)S(1)}, u32[]{:S(2)}, u32[]{:S(2)}) collective-permute-start(bf16[2,32,1,128]{3,2,1,0:T(2,128)(2,1)S(1)} %get-tuple-element.246), channel_id=1, source_target_pairs={{0,4},{4,8},{8,12},{12,0},{1,5},{5,9},{9,13},{13,1},{2,6},{6,10},{... | collective-permute-start | bytes 49160 | tf_op jit(solution)/shard_map/ppermute | solution.py:16
  150.4 4.4 %collective-permute-start.21 = (bf16[2,32,1,128]{3,2,1,0:T(2,128)(2,1)S(1)}, bf16[2,32,1,128]{3,2,1,0:T(2,128)(2,1)S(1)}, u32[]{:S(2)}, u32[]{:S(2)}) collective-permute-start(bf16[2,32,1,128]{3,2,1,0:T(2,128)(2,1)S(1)} %get-tuple-element.247), channel_id=1, source_target_pairs={{4,0},{8,4},{12,8},{0,12},{5,1},{9,5},{13,9},{1,13},{6,2},{10,6},{... | collective-permute-start | bytes 49160 | tf_op jit(solution)/shard_map/ppermute | solution.py:19
  155.1 6.5 %collective-permute-start.22 = (bf16[2,32,10,1]{3,2,1,0:T(8,128)(2,1)S(1)}, bf16[2,32,10,1]{3,2,1,0:T(8,128)(2,1)S(1)}, u32[]{:S(2)}, u32[]{:S(2)}) collective-permute-start(bf16[2,32,10,1]{3,2,1,0:T(8,128)(2,1)S(1)} %get-tuple-element.242), channel_id=1, source_target_pairs={{0,2},{2,0},{1,3},{3,1},{4,6},{6,4},{5,7},{7,5},{8,10},{10,8},{9,1... | collective-permute-start | bytes 3848 | tf_op jit(solution)/shard_map/ppermute | solution.py:16
  157.3 7.2 %collective-permute-start.23 = (bf16[2,32,10,1]{3,2,1,0:T(8,128)(2,1)S(1)}, bf16[2,32,10,1]{3,2,1,0:T(8,128)(2,1)S(1)}, u32[]{:S(2)}, u32[]{:S(2)}) collective-permute-start(bf16[2,32,10,1]{3,2,1,0:T(8,128)(2,1)S(1)} %get-tuple-element.243), channel_id=1, source_target_pairs={{2,0},{0,2},{3,1},{1,3},{6,4},{4,6},{7,5},{5,7},{10,8},{8,10},{11,... | collective-permute-start | bytes 3848 | tf_op jit(solution)/shard_map/ppermute | solution.py:19
  170.0 8.4 %collective-permute-start.24 = (bf16[2,136,2,128]{1,3,2,0:T(8,128)(2,1)S(1)}, bf16[2,136,2,128]{1,3,2,0:T(8,128)(2,1)S(1)}, u32[]{:S(2)}, u32[]{:S(2)}) collective-permute-start(bf16[2,136,2,128]{1,3,2,0:T(8,128)(2,1)S(1)} %get-tuple-element.232), channel_id=1, source_target_pairs={{0,4},{4,8},{8,12},{12,0},{1,5},{5,9},{9,13},{13,1},{2,6},{6,10},{... | collective-permute-start | bytes 417800 | tf_op jit(solution)/shard_map/ppermute | solution.py:16
  171.3 9.2 %collective-permute-start.25 = (bf16[2,136,2,128]{1,3,2,0:T(8,128)(2,1)S(1)}, bf16[2,136,2,128]{1,3,2,0:T(8,128)(2,1)S(1)}, u32[]{:S(2)}, u32[]{:S(2)}) collective-permute-start(bf16[2,136,2,128]{1,3,2,0:T(8,128)(2,1)S(1)} %get-tuple-element.233), channel_id=1, source_target_pairs={{4,0},{8,4},{12,8},{0,12},{5,1},{9,5},{13,9},{1,13},{6,2},{10,6},{... | collective-permute-start | bytes 417800 | tf_op jit(solution)/shard_map/ppermute | solution.py:19
  180.6 3.9 %collective-permute-start.26 = (bf16[2,136,12,2]{1,3,2,0:T(2,128)(2,1)S(1)}, bf16[2,136,12,2]{1,3,2,0:T(2,128)(2,1)S(1)}, u32[]{:S(2)}, u32[]{:S(2)}) collective-permute-start(bf16[2,136,12,2]{1,3,2,0:T(2,128)(2,1)S(1)} %get-tuple-element.226), channel_id=1, source_target_pairs={{0,2},{2,0},{1,3},{3,1},{4,6},{6,4},{5,7},{7,5},{8,10},{10,8},{9,1... | collective-permute-start | bytes 39176 | tf_op jit(solution)/shard_map/ppermute | solution.py:16
  180.6 4.1 %collective-permute-start.27 = (bf16[2,136,12,2]{1,3,2,0:T(2,128)(2,1)S(1)}, bf16[2,136,12,2]{1,3,2,0:T(2,128)(2,1)S(1)}, u32[]{:S(2)}, u32[]{:S(2)}) collective-permute-start(bf16[2,136,12,2]{1,3,2,0:T(2,128)(2,1)S(1)} %get-tuple-element.227), channel_id=1, source_target_pairs={{2,0},{0,2},{3,1},{1,3},{6,4},{4,6},{7,5},{5,7},{10,8},{8,10},{11,... | collective-permute-start | bytes 39176 | tf_op jit(solution)/shard_map/ppermute | solution.py:19
  199.0 11.1 %collective-permute-start.28 = (bf16[2,136,4,128]{1,2,3,0:T(4,128)(2,1)S(1)}, bf16[2,136,4,128]{1,2,3,0:T(4,128)(2,1)S(1)}, u32[]{:S(2)}, u32[]{:S(2)}) collective-permute-start(bf16[2,136,4,128]{1,2,3,0:T(4,128)(2,1)S(1)} %get-tuple-element.230), channel_id=1, source_target_pairs={{0,4},{4,8},{8,12},{12,0},{1,5},{5,9},{9,13},{13,1},{2,6},{6,10},{... | collective-permute-start | bytes 835592 | tf_op jit(solution)/shard_map/ppermute | solution.py:16
  200.2 14.8 %collective-permute-start.29 = (bf16[2,136,4,128]{1,2,3,0:T(4,128)(2,1)S(1)}, bf16[2,136,4,128]{1,2,3,0:T(4,128)(2,1)S(1)}, u32[]{:S(2)}, u32[]{:S(2)}) collective-permute-start(bf16[2,136,4,128]{1,2,3,0:T(4,128)(2,1)S(1)} %get-tuple-element.231), channel_id=1, source_target_pairs={{4,0},{8,4},{12,8},{0,12},{5,1},{9,5},{13,9},{1,13},{6,2},{10,6},{... | collective-permute-start | bytes 835592 | tf_op jit(solution)/shard_map/ppermute | solution.py:19
  215.0 4.3 %collective-permute-start.30 = (bf16[2,136,16,4]{1,2,3,0:T(8,128)(2,1)S(1)}, bf16[2,136,16,4]{1,2,3,0:T(8,128)(2,1)S(1)}, u32[]{:S(2)}, u32[]{:S(2)}) collective-permute-start(bf16[2,136,16,4]{1,2,3,0:T(8,128)(2,1)S(1)} %get-tuple-element.222), channel_id=1, source_target_pairs={{0,2},{2,0},{1,3},{3,1},{4,6},{6,4},{5,7},{7,5},{8,10},{10,8},{9,1... | collective-permute-start | bytes 104456 | tf_op jit(solution)/shard_map/ppermute | solution.py:16
  215.1 5.0 %collective-permute-start.31 = (bf16[2,136,16,4]{1,2,3,0:T(8,128)(2,1)S(1)}, bf16[2,136,16,4]{1,2,3,0:T(8,128)(2,1)S(1)}, u32[]{:S(2)}, u32[]{:S(2)}) collective-permute-start(bf16[2,136,16,4]{1,2,3,0:T(8,128)(2,1)S(1)} %get-tuple-element.223), channel_id=1, source_target_pairs={{2,0},{0,2},{3,1},{1,3},{6,4},{4,6},{7,5},{5,7},{10,8},{8,10},{11,... | collective-permute-start | bytes 104456 | tf_op jit(solution)/shard_map/ppermute | solution.py:19
  (23 other events, 125.4 us)
